TPU v7x, 32 devices: a whole 2x2x4 slice. The times are simulated.
32 devices in a mesh: batch: 8 (over z, x), head: 4 (over y, core).
Axes of the slice: x: 2, y: 2, z: 4, core: 2. Of those that a mesh axis runs over, the one named last changes fastest.
Arguments:
- tokens: bfloat16 [16384, 768], P(('batch', 'head')), may hold values from -6 to 6
- cotangent: bfloat16 [16384, 768], P(('batch', 'head')), may hold values from -6 to 6
- lengths: int32 [8, 3], P('batch'), may hold values from 1 to 1024, 2048 in all within a row
- input_weight: float32 [2304, 768], P(('batch', 'head')), may hold values from -0.21875 to 0.21875
- output_weight: float32 [768, 768], P(('batch', 'head')), may hold values from -0.875 to 0.875
- expand_weight: float32 [3072, 768], P(('batch', 'head')), may hold values from -0.21875 to 0.21875
- contract_weight: float32 [768, 3072], P(('batch', 'head')), may hold values from -0.109375 to 0.109375
- vector_params: float32 [9216], replicated, may hold values from -0.8 to 1.6, as said below
- input_first: float32 [2304, 768], P(('batch', 'head')), may hold values from -0.005859375 to 0.005859375
- input_second: float32 [2304, 768], P(('batch', 'head')), may hold values from 1.4128508e-07 to 5.6514034e-07
- output_first: float32 [768, 768], P(('batch', 'head')), may hold values from -0.005859375 to 0.005859375
- output_second: float32 [768, 768], P(('batch', 'head')), may hold values from 1.4128508e-07 to 5.6514034e-07
- expand_first: float32 [3072, 768], P(('batch', 'head')), may hold values from -0.005859375 to 0.005859375
- expand_second: float32 [3072, 768], P(('batch', 'head')), may hold values from 1.4128508e-07 to 5.6514034e-07
- contract_first: float32 [768, 3072], P(('batch', 'head')), may hold values from -0.005859375 to 0.005859375
- contract_second: float32 [768, 3072], P(('batch', 'head')), may hold values from 1.4128508e-07 to 5.6514034e-07
- vector_first: float32 [9216], replicated, may hold values from -0.0234375 to 0.0234375
- vector_second: float32 [9216], replicated, may hold values from 2.2605614e-06 to 9.042245e-06
Outputs:
- block_out: bfloat16 [16384, 768], P(('batch', 'head'))
- input_grad: bfloat16 [16384, 768], P(('batch', 'head'))
- grad_norm: float32 [], replicated
- matrix_norms: float32 [8], replicated
- input_first_new: float32 [2304, 768], P(('batch', 'head'))
- input_second_new: float32 [2304, 768], P(('batch', 'head'))
- input_weight_new: float32 [2304, 768], P(('batch', 'head'))
- input_weight_low: bfloat16 [2304, 768], P(('batch', 'head'))
- output_first_new: float32 [768, 768], P(('batch', 'head'))
- output_second_new: float32 [768, 768], P(('batch', 'head'))
- output_weight_new: float32 [768, 768], P(('batch', 'head'))
- output_weight_low: bfloat16 [768, 768], P(('batch', 'head'))
- expand_first_new: float32 [3072, 768], P(('batch', 'head'))
- expand_second_new: float32 [3072, 768], P(('batch', 'head'))
- expand_weight_new: float32 [3072, 768], P(('batch', 'head'))
- expand_weight_low: bfloat16 [3072, 768], P(('batch', 'head'))
- contract_first_new: float32 [768, 3072], P(('batch', 'head'))
- contract_second_new: float32 [768, 3072], P(('batch', 'head'))
- contract_weight_new: float32 [768, 3072], P(('batch', 'head'))
- contract_weight_low: bfloat16 [768, 3072], P(('batch', 'head'))
- vector_first_new: float32 [9216], replicated
- vector_second_new: float32 [9216], replicated
- vector_params_new: float32 [9216], replicated
Inputs may be any that keep to these rules, and one draw needn't show every extreme that they name: Each row holds 3 lengths summing to 2048; the longest in every row is exactly half of 2048. `vector_params`: entries 0 to 767 and 1536 to 2303 are norm gains near 1; the rest are shifts and biases.
All inputs are finite; a program needn't handle non-finite values.
Results may differ from a plain program's by a relative error of at most 0.012.
Values may be sent and summed in bfloat16 or wider, within the bound.
No kernel may reach another device: no remote copies, remote signals or barrier semaphores. Data moves between devices by JAX's collectives and lax.ppermute only.
A program may use at most 192 MiB of HBM per device.

v0:
```python
from functools import partial
import jax
import jax.numpy as jnp
from jax import lax
from jax.sharding import PartitionSpec as P

D = 768
HD = 64
FF = 3072
STEP = 5
NORM_EPS = 1e-05
ADAM_EPS = 1e-06
DECAY_RATE = 0.01
MATRIX_RATE = 0.5
VECTOR_RATE = 0.1


def layer_norm(values, gain_vec, bias_vec):
    row_mean = jnp.mean(values, axis=-1, keepdims=True)
    centered = values - row_mean
    variance = jnp.mean(centered * centered, axis=-1, keepdims=True)
    return centered * lax.rsqrt(variance + NORM_EPS) * gain_vec + bias_vec


def unpack_vector(params):
    pieces = [params[position * D : (position + 1) * D] for position in range(8)]
    return pieces + [params[8 * D : 8 * D + FF]]


def masked_scores(query_block, key_rows, segment, offset, block_rows, score_scale):
    scores = (
        jnp.einsum("qhd,khd->hqk", query_block, key_rows, preferred_element_type=jnp.float32)
        * score_scale
    )
    query_pos = offset + jnp.arange(block_rows, dtype=jnp.int32)
    key_pos = jnp.arange(key_rows.shape[0], dtype=jnp.int32)
    query_seg = lax.dynamic_slice_in_dim(segment, offset, block_rows, 0)
    allowed = (key_pos[None, :] <= query_pos[:, None]) & (query_seg[:, None] == segment[None, :])
    return jnp.where(allowed[None], scores, -1e30)


def head_forward(head_inputs, segment, block_count, block_rows, score_scale):
    group_rows = head_inputs.shape[1]
    heads_here = head_inputs.shape[2] // HD
    queries = head_inputs[0].reshape(group_rows, heads_here, HD)
    key_rows = head_inputs[1].reshape(group_rows, heads_here, HD)
    value_rows = head_inputs[2].reshape(group_rows, heads_here, HD)

    def one_block(block_index):
        offset = block_index * block_rows
        query_block = lax.dynamic_slice_in_dim(queries, offset, block_rows, 0)
        scores = masked_scores(query_block, key_rows, segment, offset, block_rows, score_scale)
        row_max = jnp.max(scores, axis=-1, keepdims=True)
        exponent = jnp.exp(scores - row_max)
        row_total = jnp.sum(exponent, axis=-1, keepdims=True)
        soft_weights = (exponent / row_total).astype(jnp.bfloat16)
        attended = jnp.einsum(
            "hqk,khd->qhd", soft_weights, value_rows, preferred_element_type=jnp.float32
        )
        return (attended.astype(jnp.bfloat16), row_max + jnp.log(row_total))

    attended, log_totals = lax.map(one_block, jnp.arange(block_count, dtype=jnp.int32))
    return (attended.reshape(group_rows, heads_here * HD), log_totals)


def head_backward(
    head_inputs, grad_heads, log_totals, segment, block_count, block_rows, score_scale
):
    group_rows = head_inputs.shape[1]
    heads_here = head_inputs.shape[2] // HD
    queries = head_inputs[0].reshape(group_rows, heads_here, HD)
    key_rows = head_inputs[1].reshape(group_rows, heads_here, HD)
    value_rows = head_inputs[2].reshape(group_rows, heads_here, HD)
    grad_out = grad_heads.reshape(group_rows, heads_here, HD)

    def one_block(state_pair, scan_item):
        grad_keys, grad_values = state_pair
        block_index, block_logs = scan_item
        offset = block_index * block_rows
        query_block = lax.dynamic_slice_in_dim(queries, offset, block_rows, 0)
        grad_block = lax.dynamic_slice_in_dim(grad_out, offset, block_rows, 0)
        scores = masked_scores(query_block, key_rows, segment, offset, block_rows, score_scale)
        probs = jnp.exp(scores - block_logs)
        grad_values = grad_values + jnp.einsum(
            "hqk,qhd->khd",
            probs.astype(jnp.bfloat16),
            grad_block,
            preferred_element_type=jnp.float32,
        )
        grad_probs = jnp.einsum(
            "qhd,khd->hqk", grad_block, value_rows, preferred_element_type=jnp.float32
        )
        row_delta = jnp.sum(probs * grad_probs, axis=-1, keepdims=True)
        grad_scores = (probs * (grad_probs - row_delta)).astype(jnp.bfloat16)
        grad_queries = (
            jnp.einsum("hqk,khd->qhd", grad_scores, key_rows, preferred_element_type=jnp.float32)
            * score_scale
        )
        grad_keys = (
            grad_keys
            + jnp.einsum(
                "hqk,qhd->khd", grad_scores, query_block, preferred_element_type=jnp.float32
            )
            * score_scale
        )
        return ((grad_keys, grad_values), grad_queries)

    zero_state = jnp.zeros((group_rows, heads_here, HD), jnp.float32)
    final_state, grad_queries = lax.scan(
        one_block, (zero_state, zero_state), (jnp.arange(block_count, dtype=jnp.int32), log_totals)
    )
    width_here = heads_here * HD
    stacked = jnp.stack(
        [
            grad_queries.reshape(group_rows, width_here),
            final_state[0].reshape(group_rows, width_here),
            final_state[1].reshape(group_rows, width_here),
        ]
    )
    return stacked.astype(jnp.bfloat16)


def adam_direction(gradient, first_old, second_old, master, clip_factor):
    clipped = gradient * clip_factor
    first_new = 0.5 * first_old + 0.5 * clipped
    second_new = 0.5 * second_old + 0.5 * clipped * clipped
    correction = 1.0 - 0.5**STEP
    direction = (
        first_new / correction / (jnp.sqrt(second_new / correction) + ADAM_EPS)
        + DECAY_RATE * master
    )
    return (first_new, second_new, direction)


def on_device(
    tokens,
    cotangent,
    lengths,
    input_weight,
    output_weight,
    expand_weight,
    contract_weight,
    vector_params,
    input_first,
    input_second,
    output_first,
    output_second,
    expand_first,
    expand_second,
    contract_first,
    contract_second,
    vector_first,
    vector_second,
):
    head_count = lax.axis_size("head")
    local_rows = tokens.shape[0]
    group_rows = local_rows * head_count
    block_rows = min(512, group_rows)
    block_count = group_rows // block_rows
    score_scale = HD ** (-0.5)
    (
        gain_one,
        bias_one,
        gain_two,
        bias_two,
        bias_query,
        bias_value,
        bias_output,
        bias_contract,
        bias_expand,
    ) = unpack_vector(vector_params)
    full_input, full_output, full_expand, full_contract = (
        lax.all_gather(input_weight.astype(jnp.bfloat16), ("batch", "head"), axis=0, tiled=True),
        lax.all_gather(output_weight.astype(jnp.bfloat16), ("batch", "head"), axis=0, tiled=True),
        lax.all_gather(expand_weight.astype(jnp.bfloat16), ("batch", "head"), axis=0, tiled=True),
        lax.all_gather(contract_weight.astype(jnp.bfloat16), ("batch", "head"), axis=0, tiled=True),
    )
    stacked_input = full_input.reshape(3, D, D)
    doc_ends = jnp.stack(
        [jnp.sum(lengths[0, : position + 1]) for position in range(lengths.shape[1])]
    )
    positions = jnp.arange(group_rows, dtype=jnp.int32)
    segment = jnp.sum((positions[:, None] >= doc_ends[None, :]).astype(jnp.int32), axis=1)
    resid_in = tokens.astype(jnp.float32)
    normed_one = layer_norm(resid_in, gain_one, bias_one).astype(jnp.bfloat16)
    input_bias = jnp.stack([bias_query, jnp.zeros_like(bias_query), bias_value])[:, None, :]
    projected = (
        jnp.einsum("td,cod->cto", normed_one, stacked_input, preferred_element_type=jnp.float32)
        + input_bias
    ).astype(jnp.bfloat16)
    head_inputs = lax.all_to_all(projected, "head", split_axis=2, concat_axis=1, tiled=True)
    head_out, log_totals = head_forward(head_inputs, segment, block_count, block_rows, score_scale)
    attended = lax.all_to_all(head_out, "head", split_axis=0, concat_axis=1, tiled=True)
    branch = (
        jnp.einsum("tc,oc->to", attended, full_output, preferred_element_type=jnp.float32)
        + bias_output
    )
    resid_mid = resid_in + branch
    normed_two = layer_norm(resid_mid, gain_two, bias_two).astype(jnp.bfloat16)
    expanded = (
        jnp.einsum("td,fd->tf", normed_two, full_expand, preferred_element_type=jnp.float32)
        + bias_expand
    )
    activated = jax.nn.gelu(expanded, approximate=True).astype(jnp.bfloat16)
    block_out = (
        resid_mid
        + jnp.einsum("tf,of->to", activated, full_contract, preferred_element_type=jnp.float32)
        + bias_contract
    ).astype(jnp.bfloat16)
    upstream = cotangent.astype(jnp.float32)
    grad_contract = jnp.einsum(
        "to,tf->of", cotangent, activated, preferred_element_type=jnp.float32
    )
    grad_activated = jnp.einsum(
        "to,of->tf", cotangent, full_contract, preferred_element_type=jnp.float32
    )
    unused_gelu, gelu_pull = jax.vjp(partial(jax.nn.gelu, approximate=True), expanded)
    grad_expanded = gelu_pull(grad_activated)[0].astype(jnp.bfloat16)
    grad_expand = jnp.einsum(
        "tf,td->fd", grad_expanded, normed_two, preferred_element_type=jnp.float32
    )
    grad_normed_two = jnp.einsum(
        "tf,fd->td", grad_expanded, full_expand, preferred_element_type=jnp.float32
    )
    unused_second, norm_pull_two = jax.vjp(layer_norm, resid_mid, gain_two, bias_two)
    grad_mid_norm, grad_gain_two, grad_bias_two = norm_pull_two(grad_normed_two)
    grad_mid = upstream + grad_mid_norm
    grad_branch = grad_mid.astype(jnp.bfloat16)
    grad_output = jnp.einsum("to,tc->oc", grad_branch, attended, preferred_element_type=jnp.float32)
    grad_attended = jnp.einsum(
        "to,oc->tc", grad_branch, full_output, preferred_element_type=jnp.float32
    ).astype(jnp.bfloat16)
    grad_heads = lax.all_to_all(grad_attended, "head", split_axis=1, concat_axis=0, tiled=True)
    grad_projected_heads = head_backward(
        head_inputs, grad_heads, log_totals, segment, block_count, block_rows, score_scale
    )
    grad_projected = lax.all_to_all(
        grad_projected_heads, "head", split_axis=1, concat_axis=2, tiled=True
    )
    grad_input = jnp.einsum(
        "cto,td->cod", grad_projected, normed_one, preferred_element_type=jnp.float32
    ).reshape(3 * D, D)
    grad_normed_one = jnp.einsum(
        "cto,cod->td", grad_projected, stacked_input, preferred_element_type=jnp.float32
    )
    unused_first, norm_pull_one = jax.vjp(layer_norm, resid_in, gain_one, bias_one)
    grad_in_norm, grad_gain_one, grad_bias_one = norm_pull_one(grad_normed_one)
    input_grad = (grad_mid + grad_in_norm).astype(jnp.bfloat16)
    projected_sums = jnp.sum(grad_projected.astype(jnp.float32), axis=1)
    vector_local = jnp.concatenate(
        [
            grad_gain_one,
            grad_bias_one,
            grad_gain_two,
            grad_bias_two,
            projected_sums[0],
            projected_sums[2],
            jnp.sum(grad_branch.astype(jnp.float32), axis=0),
            jnp.sum(upstream, axis=0),
            jnp.sum(grad_expanded.astype(jnp.float32), axis=0),
        ]
    )
    shard_grads = (
        lax.psum_scatter(grad_input, ("batch", "head"), scatter_dimension=0, tiled=True),
        lax.psum_scatter(grad_output, ("batch", "head"), scatter_dimension=0, tiled=True),
        lax.psum_scatter(grad_expand, ("batch", "head"), scatter_dimension=0, tiled=True),
        lax.psum_scatter(grad_contract, ("batch", "head"), scatter_dimension=0, tiled=True),
    )
    vector_grads = lax.psum(vector_local, ("batch", "head"))
    masters = (input_weight, output_weight, expand_weight, contract_weight)
    firsts = (input_first, output_first, expand_first, contract_first)
    seconds = (input_second, output_second, expand_second, contract_second)
    local_grad_sq = jnp.sum(
        jnp.stack([jnp.sum(piece_grad * piece_grad) for piece_grad in shard_grads])
    )
    weight_sq = jnp.stack([jnp.sum(master * master) for master in masters])
    grad_total = lax.psum(local_grad_sq, ("batch", "head"))
    grad_norm = jnp.sqrt(grad_total + jnp.sum(vector_grads * vector_grads))
    clip_factor = jnp.minimum(1.0, 1.0 / grad_norm)
    updated = [
        adam_direction(piece_grad, first_old, second_old, master, clip_factor)
        for piece_grad, first_old, second_old, master in zip(shard_grads, firsts, seconds, masters)
    ]
    update_sq = jnp.stack([jnp.sum(entry[2] * entry[2]) for entry in updated])
    weight_total, update_total = lax.psum((weight_sq, update_sq), ("batch", "head"))
    weight_norms = jnp.sqrt(weight_total)
    update_norms = jnp.sqrt(update_total)
    matrix_norms = jnp.concatenate([weight_norms, update_norms])
    results = []
    for position in range(4):
        first_new, second_new, direction = updated[position]
        new_master = (
            masters[position]
            - MATRIX_RATE * (weight_norms[position] / update_norms[position]) * direction
        )
        results.append((first_new, second_new, new_master, new_master.astype(jnp.bfloat16)))
    vector_first_new, vector_second_new, vector_direction = adam_direction(
        vector_grads, vector_first, vector_second, vector_params, clip_factor
    )
    vector_new = vector_params - VECTOR_RATE * vector_direction
    return (
        block_out,
        input_grad,
        grad_norm,
        matrix_norms,
        results[0][0],
        results[0][1],
        results[0][2],
        results[0][3],
        results[1][0],
        results[1][1],
        results[1][2],
        results[1][3],
        results[2][0],
        results[2][1],
        results[2][2],
        results[2][3],
        results[3][0],
        results[3][1],
        results[3][2],
        results[3][3],
        vector_first_new,
        vector_second_new,
        vector_new,
    )


def solution(mesh):
    placed = (
        P(("batch", "head"), None),
        P(("batch", "head"), None),
        P("batch", None),
        P(("batch", "head"), None),
        P(("batch", "head"), None),
        P(("batch", "head"), None),
        P(("batch", "head"), None),
        P(),
        P(("batch", "head"), None),
        P(("batch", "head"), None),
        P(("batch", "head"), None),
        P(("batch", "head"), None),
        P(("batch", "head"), None),
        P(("batch", "head"), None),
        P(("batch", "head"), None),
        P(("batch", "head"), None),
        P(),
        P(),
    )
    return jax.shard_map(
        on_device,
        mesh=mesh,
        in_specs=placed,
        out_specs=(
            P(("batch", "head"), None),
            P(("batch", "head"), None),
            P(),
            P(),
            P(("batch", "head"), None),
            P(("batch", "head"), None),
            P(("batch", "head"), None),
            P(("batch", "head"), None),
            P(("batch", "head"), None),
            P(("batch", "head"), None),
            P(("batch", "head"), None),
            P(("batch", "head"), None),
            P(("batch", "head"), None),
            P(("batch", "head"), None),
            P(("batch", "head"), None),
            P(("batch", "head"), None),
            P(("batch", "head"), None),
            P(("batch", "head"), None),
            P(("batch", "head"), None),
            P(("batch", "head"), None),
            P(),
            P(),
            P(),
        ),
        check_vma=False,
    )
```

profile of v0, /device:TPU:0, one launch (start us, length us, event | category | flops | bytes accessed | tf_op | source)
XLA Modules:
  0.0 1045.3 jit_solution(83864289830116474)
XLA Ops:
  17.2 57.2 %all-gather.5.cloned.1.call-done = bf16[2304,768]{1,0:T(8,128)(2,1)} async-done(((bf16[72,768]{1,0:T(8,128)(2,1)}), bf16[2304,768]{1,0:T(8,128)(2,1)}) %all-gather.5.cloned.1.call-update) | async-done | bytes 3538960 | tf_op jit(solution)/shard_map/all_gather | solution.py:173
  91.0 35.5 %all-to-all-done = bf16[3,512,768]{1,0,2:T(4,128)(2,1)S(1)} async-done(((bf16[3,512,768]{1,0,2:T(4,128)(2,1)}), bf16[3,512,768]{1,0,2:T(4,128)(2,1)S(1)}, u32[]{:S(2)}, u32[]{:S(2)}) %all-to-all-start) | async-done | bytes 2359328 | tf_op jit(solution)/shard_map/all_to_all | solution.py:191
  130.9 90.2 %while.27 = (s32[]{:T(128)}, bf16[4,512,3,64]{1,3,2,0:T(8,128)(2,1)}, f32[4,3,512,1]{2,1,3,0:T(4,128)S(1)}, s32[4]{0:T(128)S(1)}, s32[2048]{0:T(1024)S(1)}, /*in...) while((s32[]{:T(128)}, ...), condition=%wide.region_8.9_spmd, body=%wide.region_5.8_spmd.sunk | while | flops 846298112 | bytes 43983052 | solution.py:62
  168.7 7.3 fusion.142
  191.2 7.3 fusion.142
  213.8 7.3 fusion.142
  226.2 12.5 %all-to-all-done.1 = bf16[4,512,192]{1,2,0:T(8,128)(2,1)} async-done(((bf16[4,512,192]{1,2,0:T(8,128)(2,1)}), bf16[4,512,192]{1,2,0:T(8,128)(2,1)}, u32[]{:S(2)}, u32[]{:S(2)}) %all-to-all-start.1) | async-done | bytes 786464 | tf_op jit(solution)/shard_map/all_to_all | solution.py:193
  242.7 8.6 fusion.72
  251.4 13.3 %all-gather.11.cloned.1.call-done = bf16[768,3072]{1,0:T(8,128)(2,1)} async-done(((bf16[24,3072]{1,0:T(8,128)(2,1)}), bf16[768,3072]{1,0:T(8,128)(2,1)}) %all-gather.11.cloned.1.call-update) | async-done | bytes 4718608 | tf_op jit(solution)/shard_map/all_gather | solution.py:176
  264.7 10.3 convert_reduce_fusion
  291.2 7.9 all-to-all-done.2
  303.4 140.5 %while.28 = (s32[]{:T(128)}, f32[2048,3,64]{0,2,1:T(8,128)}, f32[2048,3,64]{0,2,1:T(8,128)}, bf16[4,512,3,64]{1,3,2,0:T(8,128)(2,1)}, s32[4]{0:T(128)S(1)}, /*in...) while((s32[]{:T(128)}, f32[2048,3,64]{0,2,1:T(8,128)}, ...), condition=%wide.region_15.16_spmd.clone, body=%wide.region_13.15_spmd.clone.sunk | while | flops 2065660928 | bytes 219607728 | solution.py:109
  309.7 7.3 multiply_reduce_fusion.18
  455.0 53.8 %all_to_all.68 = bf16[3,2048,192]{2,0,1:T(4,128)(2,1)} all-to-all(bf16[3,2048,192]{2,0,1:T(4,128)(2,1)} %copy.155), channel_id=1, replica_groups=mesh['batch'=8,'head'=4] {'head'}, dimensions={1} | all-to-all | bytes 4718592 | tf_op jit(solution)/shard_map/all_to_all | solution.py:237
  520.8 10.0 convolution_bitcast_fusion
  530.9 9.9 copy.165
  542.3 8.5 fusion.71
  550.7 7.5 copy.163
  569.5 68.4 %reduce-scatter.7.cloned.1.call-done = f32[72,768]{1,0:T(8,128)} async-done(((f32[2304,768]{1,0:T(8,128)}), f32[72,768]{1,0:T(8,128)}) %reduce-scatter.7.cloned.1.call-update) | async-done | bytes 221200 | tf_op jit(solution)/shard_map/reduce_scatter | solution.py:264
  640.8 137.8 %reduce-scatter.13.cloned.1.call-done = f32[24,3072]{1,0:T(8,128)} async-done(((f32[768,3072]{1,0:T(8,128)}), f32[24,3072]{1,0:T(8,128)}) %reduce-scatter.13.cloned.1.call-update) | async-done | bytes 294928 | tf_op jit(solution)/shard_map/reduce_scatter | solution.py:267
  781.0 138.9 %reduce-scatter.11.cloned.1.call-done = f32[96,768]{1,0:T(8,128)} async-done(((f32[3072,768]{1,0:T(8,128)}), f32[96,768]{1,0:T(8,128)}) %reduce-scatter.11.cloned.1.call-update) | async-done | bytes 294928 | tf_op jit(solution)/shard_map/reduce_scatter | solution.py:266
  923.0 9.2 add_convert_fusion.2
  932.2 40.5 %all-reduce.1 = (f32[]{:T(128)}, f32[9216]{0:T(1024)S(1)}) all-reduce(f32[]{:T(128)S(6)} %reduce_sum.388, f32[9216]{0:T(1024)S(1)} %constant_dynamic-update-slice_fusion), channel_id=1, replica_groups=mesh['batch'=8,'head'=4] {'batch','head'}, use_global_device_ids=true, to_apply=%region_26.27 | all-reduce | flops 9217 | bytes 73736 | tf_op jit(solution)/shard_map/psum | solution.py:277
  986.5 39.3 %all-reduce = (f32[4]{0:T(128)S(1)}, f32[4]{0:T(128)S(1)}) all-reduce(f32[4]{0:T(128)S(1)} %get-tuple-element.418, f32[4]{0:T(128)S(1)} %get-tuple-element.417), channel_id=1, replica_groups=mesh['batch'=8,'head'=4] {'batch','head'}, use_global_device_ids=true, to_apply=%region_46.47 | all-reduce | flops 8 | bytes 64 | tf_op jit(solution)/shard_map/psum | solution.py:285
  (451 shorter events, 314.1 us)
Async XLA Ops:
  7.2 67.2 %all-gather.5.cloned.1.call-start = ((), (), s32[]{:S(2)}) async-start(), calls=%async_computation.8 | async-start | bytes 3649536 | tf_op jit(solution)/shard_map/all_gather | solution.py:173
  8.9 217.4 %all-gather.7.cloned.1.call-start = ((), (), s32[]{:S(2)}) async-start(), calls=%async_computation.9 | async-start | bytes 1216512 | tf_op jit(solution)/shard_map/all_gather | solution.py:174
  10.4 232.3 %all-gather.9.cloned.1.call-start = ((), (), s32[]{:S(2)}) async-start(), calls=%async_computation.10 | async-start | bytes 4866048 | tf_op jit(solution)/shard_map/all_gather | solution.py:175
  13.6 65.2 %copy-start.49 = (f32[768]{0:T(1024)}, f32[768]{0:T(1024)S(1)}, u32[]{:S(2)}) copy-start(f32[768]{0:T(1024)S(1)} %get-tuple-element.403) | copy-start | bytes 9220
  13.6 65.2 %copy-start.74 = (f32[768]{0:T(1024)}, f32[768]{0:T(1024)S(1)}, u32[]{:S(2)}) copy-start(f32[768]{0:T(1024)S(1)} %get-tuple-element.402) | copy-start | bytes 9220
  15.0 63.8 %copy-start.53 = (f32[512]{0:T(512)}, f32[512]{0:T(512)S(1)}, u32[]{:S(2)}) copy-start(f32[512]{0:T(512)S(1)} %broadcast_multiply_fusion.1) | copy-start | bytes 6148
  17.1 61.7 %copy-start.55 = (f32[512]{0:T(512)}, f32[512]{0:T(512)S(1)}, u32[]{:S(2)}) copy-start(f32[512]{0:T(512)S(1)} %fusion.65) | copy-start | bytes 6148
  83.2 43.4 %all-to-all-start = ((bf16[3,512,768]{1,0,2:T(4,128)(2,1)}), bf16[3,512,768]{1,0,2:T(4,128)(2,1)S(1)}, u32[]{:S(2)}, u32[]{:S(2)}) async-start(bf16[3,512,768]{1,0,2:T(4,128)(2,1)} %copy.147), calls=%async_computation | async-start | bytes 6291456 | tf_op jit(solution)/shard_map/all_to_all | solution.py:191
  87.0 177.7 %all-gather.11.cloned.1.call-start = ((), (), s32[]{:S(2)}) async-start(), calls=%async_computation.11 | async-start | bytes 4866048 | tf_op jit(solution)/shard_map/all_gather | solution.py:176
  130.9 107.8 %copy-start.9 = (bf16[512,768]{1,0:T(8,128)(2,1)S(1)}, bf16[512,768]{1,0:T(8,128)(2,1)}, u32[]{:S(2)}) copy-start(bf16[512,768]{1,0:T(8,128)(2,1)} %param.22) | copy-start | bytes 2359300
  130.9 107.8 %copy-start.76 = (f32[768]{0:T(1024)S(1)}, f32[768]{0:T(1024)}, u32[]{:S(2)}) copy-start(f32[768]{0:T(1024)} %get-tuple-element.399) | copy-start | bytes 9220
  221.1 17.6 %all-to-all-start.1 = ((bf16[4,512,192]{1,2,0:T(8,128)(2,1)}), bf16[4,512,192]{1,2,0:T(8,128)(2,1)}, u32[]{:S(2)}, u32[]{:S(2)}) async-start(bf16[4,512,192]{1,2,0:T(8,128)(2,1)} %bitcast.161), calls=%async_computation.1 | async-start | bytes 1572864 | tf_op jit(solution)/shard_map/all_to_all | solution.py:193
  284.0 15.1 %all-to-all-start.2 = ((bf16[512,4,192]{0,2,1:T(8,128)(2,1)}), bf16[512,4,192]{0,2,1:T(8,128)(2,1)S(1)}, u32[]{:S(2)}, u32[]{:S(2)}) async-start(bf16[512,4,192]{0,2,1:T(8,128)(2,1)} %bitcast.156), calls=%async_computation.2 | async-start | bytes 1572864 | tf_op jit(solution)/shard_map/all_to_all | solution.py:233
  287.5 280.4 %reduce-scatter.9.cloned.1.call-start = ((), (), s32[]{:S(2)}) async-start(), calls=%async_computation.13 | async-start | bytes 2433024 | tf_op jit(solution)/shard_map/reduce_scatter | solution.py:265
  291.1 346.7 %reduce-scatter.7.cloned.1.call-start = ((), (), s32[]{:S(2)}) async-start(), calls=%async_computation.12 | async-start | bytes 7299072 | tf_op jit(solution)/shard_map/reduce_scatter | solution.py:264
  519.7 258.9 %reduce-scatter.13.cloned.1.call-start = ((), (), s32[]{:S(2)}) async-start(), calls=%async_computation.15 | async-start | bytes 9732096 | tf_op jit(solution)/shard_map/reduce_scatter | solution.py:267
  540.8 379.1 %reduce-scatter.11.cloned.1.call-start = ((), (), s32[]{:S(2)}) async-start(), calls=%async_computation.14 | async-start | bytes 9732096 | tf_op jit(solution)/shard_map/reduce_scatter | solution.py:266
  567.8 355.1 %copy-start.16 = (f32[512,768]{1,0:T(8,128)S(1)}, f32[512,768]{1,0:T(8,128)}, u32[]{:S(2)}) copy-start(f32[512,768]{1,0:T(8,128)} %copy-done.13) | copy-start | bytes 4718596
  567.8 355.1 %copy-start.71 = (f32[768]{0:T(1024)S(1)}, f32[768]{0:T(1024)}, u32[]{:S(2)}) copy-start(f32[768]{0:T(1024)} %get-tuple-element.404) | copy-start | bytes 9220
  932.2 100.8 %copy-start.46 = (f32[9216]{0:T(1024)S(1)}, f32[9216]{0:T(1024)}, u32[]{:S(2)}) copy-start(f32[9216]{0:T(1024)} %param.29) | copy-start | bytes 110596
  932.2 100.8 %copy-start.51 = (f32[9216]{0:T(1024)S(1)}, f32[9216]{0:T(1024)}, u32[]{:S(2)}) copy-start(f32[9216]{0:T(1024)} %param.39) | copy-start | bytes 110596
  972.8 60.3 %copy-start.52 = (f32[9216]{0:T(1024)S(1)}, f32[9216]{0:T(1024)}, u32[]{:S(2)}) copy-start(f32[9216]{0:T(1024)} %param.38) | copy-start | bytes 110596
  976.6 59.6 %copy-start.30 = (f32[24,3072]{1,0:T(8,128)}, f32[24,3072]{1,0:T(8,128)S(1)}, u32[]{:S(2)}) copy-start(f32[24,3072]{1,0:T(8,128)S(1)} %get-tuple-element.378) | copy-start | bytes 884740
  976.6 59.6 %copy-start.31 = (f32[24,3072]{1,0:T(8,128)}, f32[24,3072]{1,0:T(8,128)S(1)}, u32[]{:S(2)}) copy-start(f32[24,3072]{1,0:T(8,128)S(1)} %get-tuple-element.379) | copy-start | bytes 884740
  (114 other events, 1502.3 us)
Sparse Core Ops, SparseCore 0:
  11.5 62.8 all-gather.4
  77.9 54.3 all-gather.6
  135.7 62.6 all-gather.8
  201.7 62.9 all-gather.10
  293.3 99.1 reduce-scatter.8
  519.9 117.9 reduce-scatter.6
  643.8 134.7 reduce-scatter.12
  785.5 134.4 reduce-scatter.10
where the time goes:
time: 1050 us
  waiting for transfers between devices  472 us (45%)
  matrix products  220 us (21%)
  blocking collectives  134 us (13%)
  other arithmetic  110 us (10%)
  local copies, waits for them, and re-layouts  64.5 us (6%)
  between operations  25.8 us (2%)
  starting transfers between devices  12.5 us (1%)
    reduce_scatter x1, waiting for transfers between devices, on_device(): lax.psum_scatter(grad_expand, ('batch', 'head'), scatter_dimension=0, til...  139 us
    reduce_scatter x1, waiting for transfers between devices, on_device(): lax.psum_scatter(grad_contract, ('batch', 'head'), scatter_dimension=0, t...  138 us
    reduce_scatter x1, waiting for transfers between devices, on_device(): lax.psum_scatter(grad_input, ('batch', 'head'), scatter_dimension=0, tile...  68.4 us
    all_gather x1, waiting for transfers between devices, on_device(): lax.all_gather(input_weight.astype(jnp.bfloat16), ('batch', 'head'), axis...  57.2 us
    all_to_all x1, blocking collectives, on_device(): lax.all_to_all(grad_projected_heads, 'head', split_axis=1, concat_axis=2,...  53.8 us
    psum x1, blocking collectives, on_device(): grad_total = lax.psum(local_grad_sq, ('batch', 'head'))  40.5 us
    psum x1, blocking collectives, on_device(): lax.psum((weight_sq, update_sq), ('batch', 'head'))  39.3 us
    all_to_all x1, waiting for transfers between devices, on_device(): lax.all_to_all(projected, 'head', split_axis=2, concat_axis=1, tiled=True)  35.5 us
  transfers between devices with their start and end apart: 11, of which 8 were waited for; matrix products, arithmetic and copies ran while one was open for 32% of the time, Pallas kernels for 0%

commit v1 on v0

--- a/solution.py
+++ b/solution.py
@@ -234,8 +234,11 @@
     grad_projected_heads = head_backward(
         head_inputs, grad_heads, log_totals, segment, block_count, block_rows, score_scale
     )
-    grad_projected = lax.all_to_all(
-        grad_projected_heads, "head", split_axis=1, concat_axis=2, tiled=True
+    grad_projected = jnp.concatenate(
+        lax.all_to_all(
+            jnp.stack(jnp.split(grad_projected_heads, lax.axis_size("head"), axis=1)), "head", 0, 0
+        ),
+        axis=2,
     )
     grad_input = jnp.einsum(
         "cto,td->cod", grad_projected, normed_one, preferred_element_type=jnp.float32

time: 1050 us -> 1020 us (0.971)
  blocking collectives: 134 us -> 111 us
  local copies, waits for them, and re-layouts: 64.5 us -> 47.3 us
    all_to_all x1, blocking collectives: 53.8 us -> 31 us  [on_device(): lax.all_to_all(jnp.stack(jnp.split(grad_projected_heads, lax.axis_size('h...]
    all_to_all x2 -> x0, local copies, waits for them, and re-layouts: 13.1 us -> none  [on_device(): lax.all_to_all(grad_projected_heads, 'head', split_axis=1, concat_axis=2,...]
  transfers between devices with their start and end apart: 11 -> 11, of which waited for: 8 -> 8; matrix products, arithmetic and copies ran while one was open for 32% -> 31% of each run, Pallas kernels for 0% -> 0%
where the time goes in v1:
time: 1020 us; the launch traced here: 1010 us
  waiting for transfers between devices  480 us (47%)
  matrix products  221 us (22%)
  blocking collectives  111 us (11%)
  other arithmetic  107 us (10%)
  local copies, waits for them, and re-layouts  47.3 us (5%)
  between operations  25.7 us (3%)
  starting transfers between devices  12.8 us (1%)
    reduce_scatter x1, waiting for transfers between devices, on_device(): lax.psum_scatter(grad_expand, ('batch', 'head'), scatter_dimension=0, til...  139 us
    reduce_scatter x1, waiting for transfers between devices, on_device(): lax.psum_scatter(grad_contract, ('batch', 'head'), scatter_dimension=0, t...  138 us
    reduce_scatter x1, waiting for transfers between devices, on_device(): lax.psum_scatter(grad_input, ('batch', 'head'), scatter_dimension=0, tile...  76.6 us
    all_gather x1, waiting for transfers between devices, on_device(): lax.all_gather(input_weight.astype(jnp.bfloat16), ('batch', 'head'), axis...  57.2 us
    psum x1, blocking collectives, on_device(): grad_total = lax.psum(local_grad_sq, ('batch', 'head'))  40.9 us
    psum x1, blocking collectives, on_device(): lax.psum((weight_sq, update_sq), ('batch', 'head'))  39.3 us
    all_to_all x1, waiting for transfers between devices, on_device(): lax.all_to_all(projected, 'head', split_axis=2, concat_axis=1, tiled=True)  35.8 us
    dot_general x8, matrix products, masked_scores(): jnp.einsum('qhd,khd->hqk', query_block, key_rows, preferred_element_type=...  31.5 us
  transfers between devices with their start and end apart: 11, of which 8 were waited for; matrix products, arithmetic and copies ran while one was open for 31% of the time, Pallas kernels for 0%

profile of v1, /device:TPU:0, one launch (start us, length us, event | category | flops | bytes accessed | tf_op | source)
XLA Modules:
  0.0 1012.2 jit_solution(7820720820823793373)
XLA Ops:
  17.2 57.2 %all-gather.5.cloned.1.call-done = bf16[2304,768]{1,0:T(8,128)(2,1)} async-done(((bf16[72,768]{1,0:T(8,128)(2,1)}), bf16[2304,768]{1,0:T(8,128)(2,1)}) %all-gather.5.cloned.1.call-update) | async-done | bytes 3538960 | tf_op jit(solution)/shard_map/all_gather | solution.py:173
  90.8 35.8 %all-to-all-done = bf16[3,512,768]{1,0,2:T(4,128)(2,1)S(1)} async-done(((bf16[3,512,768]{1,0,2:T(4,128)(2,1)}), bf16[3,512,768]{1,0,2:T(4,128)(2,1)S(1)}, u32[]{:S(2)}, u32[]{:S(2)}) %all-to-all-start) | async-done | bytes 2359328 | tf_op jit(solution)/shard_map/all_to_all | solution.py:191
  130.9 90.3 %while.27 = (s32[]{:T(128)}, bf16[4,512,3,64]{1,3,2,0:T(8,128)(2,1)}, f32[4,3,512,1]{2,1,3,0:T(4,128)S(1)}, s32[4]{0:T(128)S(1)}, s32[2048]{0:T(1024)S(1)}, /*in...) while((s32[]{:T(128)}, ...), condition=%wide.region_8.9_spmd, body=%wide.region_5.8_spmd.sunk | while | flops 846298112 | bytes 43983052 | solution.py:62
  146.1 7.3 fusion.141
  168.7 7.3 fusion.141
  191.2 7.4 fusion.141
  213.8 7.3 fusion.141
  226.6 12.2 %all-to-all-done.1 = bf16[4,512,192]{1,2,0:T(8,128)(2,1)} async-done(((bf16[4,512,192]{1,2,0:T(8,128)(2,1)}), bf16[4,512,192]{1,2,0:T(8,128)(2,1)}, u32[]{:S(2)}, u32[]{:S(2)}) %all-to-all-start.1) | async-done | bytes 786464 | tf_op jit(solution)/shard_map/all_to_all | solution.py:193
  242.8 8.6 fusion.72
  251.4 13.3 %all-gather.11.cloned.1.call-done = bf16[768,3072]{1,0:T(8,128)(2,1)} async-done(((bf16[24,3072]{1,0:T(8,128)(2,1)}), bf16[768,3072]{1,0:T(8,128)(2,1)}) %all-gather.11.cloned.1.call-update) | async-done | bytes 4718608 | tf_op jit(solution)/shard_map/all_gather | solution.py:176
  264.7 10.3 %convert_reduce_fusion = (f32[3072]{0:T(1024)}, bf16[512,3072]{1,0:T(8,128)(2,1)S(1)}) fusion(f32[512,3072]{1,0:T(8,128)} %fusion.72, f32[3072]{0:T(1024)S(1)} %slice.92, bf16[512,768]{1,0:T(8,128)(2,1)S(1)} %copy-done.16, bf16[768,3072]{1,0:T(8,128)(2,1)} %all-gather.11.cloned.1.call-done), kind=kOutput, calls=%fused_computation.57 | convolution fusion | flops 2452091904 | bytes 14966784 | tf_op jit(solution)/shard_map/to,of->tf/dot_general | solution.py:214
  291.2 7.9 all-to-all-done.2
  303.4 140.8 %while.28 = (s32[]{:T(128)}, f32[2048,3,64]{0,2,1:T(8,128)}, f32[2048,3,64]{0,2,1:T(8,128)}, bf16[4,512,3,64]{1,3,2,0:T(8,128)(2,1)}, s32[4]{0:T(128)S(1)}, /*in...) while((s32[]{:T(128)}, f32[2048,3,64]{0,2,1:T(8,128)}, ...), condition=%wide.region_15.16_spmd.clone, body=%wide.region_13.15_spmd.clone.sunk | while | flops 2065660928 | bytes 219607728 | solution.py:109
  309.5 7.4 multiply_reduce_fusion.18
  448.3 31.0 %all_to_all.55 = bf16[4,3,512,192]{2,3,1,0:T(8,128)(2,1)S(1)} all-to-all(bf16[4,3,512,192]{2,3,1,0:T(8,128)(2,1)S(1)} %pad_maximum_fusion.1), channel_id=1, replica_groups=mesh['batch'=8,'head'=4] {'head'}, dimensions={0} | all-to-all | bytes 4718592 | tf_op jit(solution)/shard_map/all_to_all | solution.py:238
  486.9 10.3 %convolution_bitcast_fusion = f32[768,3072]{0,1:T(8,128)} fusion(bf16[512,768]{1,0:T(8,128)(2,1)} %param.23, f32[512,3072]{1,0:T(8,128)} %fusion.72, f32[3072]{0:T(1024)S(1)} %copy-done.65), kind=kOutput, calls=%fused_computation.59 | convolution fusion | flops 2431647744 | bytes 16527360 | tf_op jit(solution)/shard_map/to,tf->of/dot_general | solution.py:211
  497.2 9.9 copy.136
  507.9 9.0 fusion.71
  527.7 76.6 %reduce-scatter.7.cloned.1.call-done = f32[72,768]{1,0:T(8,128)} async-done(((f32[2304,768]{1,0:T(8,128)}), f32[72,768]{1,0:T(8,128)}) %reduce-scatter.7.cloned.1.call-update) | async-done | bytes 221200 | tf_op jit(solution)/shard_map/reduce_scatter | solution.py:267
  607.2 137.9 %reduce-scatter.13.cloned.1.call-done = f32[24,3072]{1,0:T(8,128)} async-done(((f32[768,3072]{1,0:T(8,128)}), f32[24,3072]{1,0:T(8,128)}) %reduce-scatter.13.cloned.1.call-update) | async-done | bytes 294928 | tf_op jit(solution)/shard_map/reduce_scatter | solution.py:270
  747.5 138.9 %reduce-scatter.11.cloned.1.call-done = f32[96,768]{1,0:T(8,128)} async-done(((f32[3072,768]{1,0:T(8,128)}), f32[96,768]{1,0:T(8,128)}) %reduce-scatter.11.cloned.1.call-update) | async-done | bytes 294928 | tf_op jit(solution)/shard_map/reduce_scatter | solution.py:269
  889.5 9.2 add_convert_fusion.2
  898.7 40.9 %all-reduce.1 = (f32[]{:T(128)}, f32[9216]{0:T(1024)S(1)}) all-reduce(f32[]{:T(128)S(6)} %reduce_sum.388, f32[9216]{0:T(1024)S(1)} %constant_dynamic-update-slice_fusion), channel_id=1, replica_groups=mesh['batch'=8,'head'=4] {'batch','head'}, use_global_device_ids=true, to_apply=%region_26.27 | all-reduce | flops 9217 | bytes 73736 | tf_op jit(solution)/shard_map/psum | solution.py:280
  953.5 39.3 %all-reduce = (f32[4]{0:T(128)S(1)}, f32[4]{0:T(128)S(1)}) all-reduce(f32[4]{0:T(128)S(1)} %get-tuple-element.399, f32[4]{0:T(128)S(1)} %get-tuple-element.398), channel_id=1, replica_groups=mesh['batch'=8,'head'=4] {'batch','head'}, use_global_device_ids=true, to_apply=%region_46.47 | all-reduce | flops 8 | bytes 64 | tf_op jit(solution)/shard_map/psum | solution.py:288
  (445 shorter events, 294.8 us)
Async XLA Ops:
  7.2 67.2 %all-gather.5.cloned.1.call-start = ((), (), s32[]{:S(2)}) async-start(), calls=%async_computation.8 | async-start | bytes 3649536 | tf_op jit(solution)/shard_map/all_gather | solution.py:173
  8.9 217.7 %all-gather.7.cloned.1.call-start = ((), (), s32[]{:S(2)}) async-start(), calls=%async_computation.9 | async-start | bytes 1216512 | tf_op jit(solution)/shard_map/all_gather | solution.py:174
  10.4 232.3 %all-gather.9.cloned.1.call-start = ((), (), s32[]{:S(2)}) async-start(), calls=%async_computation.10 | async-start | bytes 4866048 | tf_op jit(solution)/shard_map/all_gather | solution.py:175
  13.6 65.2 %copy-start.47 = (f32[768]{0:T(1024)}, f32[768]{0:T(1024)S(1)}, u32[]{:S(2)}) copy-start(f32[768]{0:T(1024)S(1)} %get-tuple-element.384) | copy-start | bytes 9220
  13.6 65.2 %copy-start.72 = (f32[768]{0:T(1024)}, f32[768]{0:T(1024)S(1)}, u32[]{:S(2)}) copy-start(f32[768]{0:T(1024)S(1)} %get-tuple-element.383) | copy-start | bytes 9220
  15.0 63.8 %copy-start.51 = (f32[512]{0:T(512)}, f32[512]{0:T(512)S(1)}, u32[]{:S(2)}) copy-start(f32[512]{0:T(512)S(1)} %broadcast_multiply_fusion.1) | copy-start | bytes 6148
  17.1 61.7 %copy-start.53 = (f32[512]{0:T(512)}, f32[512]{0:T(512)S(1)}, u32[]{:S(2)}) copy-start(f32[512]{0:T(512)S(1)} %fusion.65) | copy-start | bytes 6148
  83.1 43.4 %all-to-all-start = ((bf16[3,512,768]{1,0,2:T(4,128)(2,1)}), bf16[3,512,768]{1,0,2:T(4,128)(2,1)S(1)}, u32[]{:S(2)}, u32[]{:S(2)}) async-start(bf16[3,512,768]{1,0,2:T(4,128)(2,1)} %copy.124), calls=%async_computation | async-start | bytes 6291456 | tf_op jit(solution)/shard_map/all_to_all | solution.py:191
  87.0 177.7 %all-gather.11.cloned.1.call-start = ((), (), s32[]{:S(2)}) async-start(), calls=%async_computation.11 | async-start | bytes 4866048 | tf_op jit(solution)/shard_map/all_gather | solution.py:176
  130.9 107.9 %copy-start.9 = (bf16[512,768]{1,0:T(8,128)(2,1)S(1)}, bf16[512,768]{1,0:T(8,128)(2,1)}, u32[]{:S(2)}) copy-start(bf16[512,768]{1,0:T(8,128)(2,1)} %param.22) | copy-start | bytes 2359300
  130.9 107.9 %copy-start.74 = (f32[768]{0:T(1024)S(1)}, f32[768]{0:T(1024)}, u32[]{:S(2)}) copy-start(f32[768]{0:T(1024)} %get-tuple-element.380) | copy-start | bytes 9220
  221.2 17.6 %all-to-all-start.1 = ((bf16[4,512,192]{1,2,0:T(8,128)(2,1)}), bf16[4,512,192]{1,2,0:T(8,128)(2,1)}, u32[]{:S(2)}, u32[]{:S(2)}) async-start(bf16[4,512,192]{1,2,0:T(8,128)(2,1)} %bitcast.165), calls=%async_computation.1 | async-start | bytes 1572864 | tf_op jit(solution)/shard_map/all_to_all | solution.py:193
  284.0 15.1 %all-to-all-start.2 = ((bf16[512,4,192]{0,2,1:T(8,128)(2,1)}), bf16[512,4,192]{0,2,1:T(8,128)(2,1)S(1)}, u32[]{:S(2)}, u32[]{:S(2)}) async-start(bf16[512,4,192]{0,2,1:T(8,128)(2,1)} %bitcast.160), calls=%async_computation.2 | async-start | bytes 1572864 | tf_op jit(solution)/shard_map/all_to_all | solution.py:233
  287.5 238.6 %reduce-scatter.9.cloned.1.call-start = ((), (), s32[]{:S(2)}) async-start(), calls=%async_computation.13 | async-start | bytes 2433024 | tf_op jit(solution)/shard_map/reduce_scatter | solution.py:268
  291.2 313.1 %reduce-scatter.7.cloned.1.call-start = ((), (), s32[]{:S(2)}) async-start(), calls=%async_computation.12 | async-start | bytes 7299072 | tf_op jit(solution)/shard_map/reduce_scatter | solution.py:267
  486.2 258.9 %reduce-scatter.13.cloned.1.call-start = ((), (), s32[]{:S(2)}) async-start(), calls=%async_computation.15 | async-start | bytes 9732096 | tf_op jit(solution)/shard_map/reduce_scatter | solution.py:270
  507.2 379.3 %reduce-scatter.11.cloned.1.call-start = ((), (), s32[]{:S(2)}) async-start(), calls=%async_computation.14 | async-start | bytes 9732096 | tf_op jit(solution)/shard_map/reduce_scatter | solution.py:269
  526.0 363.4 %copy-start.15 = (f32[512,768]{1,0:T(8,128)S(1)}, f32[512,768]{1,0:T(8,128)}, u32[]{:S(2)}) copy-start(f32[512,768]{1,0:T(8,128)} %copy-done.13) | copy-start | bytes 4718596
  526.0 363.4 %copy-start.69 = (f32[768]{0:T(1024)S(1)}, f32[768]{0:T(1024)}, u32[]{:S(2)}) copy-start(f32[768]{0:T(1024)} %get-tuple-element.385) | copy-start | bytes 9220
  898.7 101.2 %copy-start.44 = (f32[9216]{0:T(1024)S(1)}, f32[9216]{0:T(1024)}, u32[]{:S(2)}) copy-start(f32[9216]{0:T(1024)} %param.29) | copy-start | bytes 110596
  898.7 101.2 %copy-start.49 = (f32[9216]{0:T(1024)S(1)}, f32[9216]{0:T(1024)}, u32[]{:S(2)}) copy-start(f32[9216]{0:T(1024)} %param.39) | copy-start | bytes 110596
  939.7 60.3 %copy-start.50 = (f32[9216]{0:T(1024)S(1)}, f32[9216]{0:T(1024)}, u32[]{:S(2)}) copy-start(f32[9216]{0:T(1024)} %param.38) | copy-start | bytes 110596
  943.5 59.6 %copy-start.28 = (f32[24,3072]{1,0:T(8,128)}, f32[24,3072]{1,0:T(8,128)S(1)}, u32[]{:S(2)}) copy-start(f32[24,3072]{1,0:T(8,128)S(1)} %get-tuple-element.357) | copy-start | bytes 884740
  943.5 59.6 %copy-start.29 = (f32[24,3072]{1,0:T(8,128)}, f32[24,3072]{1,0:T(8,128)S(1)}, u32[]{:S(2)}) copy-start(f32[24,3072]{1,0:T(8,128)S(1)} %get-tuple-element.358) | copy-start | bytes 884740
  (112 other events, 1476.2 us)
Sparse Core Ops, SparseCore 0:
  11.5 62.8 all-gather.4
  77.9 54.3 all-gather.6
  135.7 62.6 all-gather.8
  201.7 62.9 all-gather.10
  293.3 99.1 reduce-scatter.8
  486.3 117.9 reduce-scatter.6
  610.2 134.8 reduce-scatter.12
  752.0 134.4 reduce-scatter.10
